TPU v7x, 32 devices: a whole 2x2x4 slice. The times are simulated.
32 devices in a mesh: row: 16 (over z, y, x), col: 2 (over core).
Axes of the slice: x: 2, y: 2, z: 4, core: 2. Of those that a mesh axis runs over, the one named last changes fastest.
Arguments:
- panel_u: bfloat16 [16, 2560, 128], P('row'), may hold values from -0.125 to 0.125
- panel_v: bfloat16 [16, 2560, 128], P('row', 'col'), may hold values from -0.25 to 0.25
- linv: bfloat16 [2560, 2560], P('row', 'col')
- trail_u: bfloat16 [16, 4, 2560, 128], P('row', 'col'), may hold values from -0.125 to 0.125
- trail_v: bfloat16 [16, 4, 2560, 128], P('row', 'col'), may hold values from -0.125 to 0.125
- rank_map: int32 [16, 16], replicated, may hold values from 32 to 128, as said below
- tile_of_slot: int32 [16], replicated, may hold values from 0 to 15, each once
- band_cols: int32 [4], P('col'), may hold values from 0 to 15, as said below
Outputs:
- gram_left: float32 [16, 4, 256, 256], P('row', 'col')
- gram_right: float32 [16, 4, 256, 256], P('row', 'col')
Inputs may be any that keep to these rules, and one draw needn't show every extreme that they name: rank_map[i, j] for j != i is the rank of trailing tile (i, j), including band tiles with j > i, whose core is zero; rank_map[i, i] is the rank of panel tile i; some panel tile has rank 128. `tile_of_slot`: a permutation. `band_cols`: distinct values.
All inputs are finite; a program needn't handle non-finite values.
Results may differ from a plain program's by a relative error of at most 0.0049.
Values may be sent and summed in bfloat16 or wider, within the bound.
No kernel may reach another device: no remote copies, remote signals or barrier semaphores. Data moves between devices by JAX's collectives and lax.ppermute only.
A program may use at most 64 MiB of HBM per device.

v0:
```python
import jax
import jax.numpy as jnp
from jax import lax
from jax.sharding import PartitionSpec as P


def broadcast(block, axis, holder):
    block = jnp.where(lax.axis_index(axis) == holder, block, jnp.zeros_like(block))
    return lax.psum(block, axis)


def cross_rows(first, second):
    return lax.dot_general(
        first, second, (((0,), (0,)), ((), ())), preferred_element_type=jnp.float32
    )


def shards(panel_u, panel_v, linv, trail_u, trail_v, rank_map, tile_of_slot, band_cols):
    tile_count = tile_of_slot.shape[0]
    rank_width = panel_u.shape[2]
    band_width = band_cols.shape[0]
    slot_ids = jnp.arange(tile_count, dtype=jnp.int32)
    row_ids = slot_ids[:, None]
    col_ids = slot_ids[None, :]
    columns = jnp.arange(rank_width, dtype=jnp.int32)

    def rank_lookup(first_tile, second_tile):
        return jnp.sum(jnp.where((row_ids == first_tile) & (col_ids == second_tile), rank_map, 0))

    own_slot = lax.axis_index("row")
    own_tile = jnp.sum(jnp.where(slot_ids == own_slot, tile_of_slot, 0))
    own_keep = (columns < rank_lookup(own_tile, own_tile))[None, :]
    own_basis = jnp.where(own_keep, panel_u[0], jnp.zeros_like(panel_u[0]))
    own_right = jnp.where(own_keep, panel_v[0], jnp.zeros_like(panel_v[0]))
    band_tiles = [band_cols[band_slot] for band_slot in range(band_width)]
    sources = [
        jnp.sum(jnp.where(tile_of_slot == band_tile, slot_ids, 0)) for band_tile in band_tiles
    ]
    partial_value = jnp.dot(
        lax.all_gather(linv, "row", axis=0, tiled=True),
        own_right,
        preferred_element_type=jnp.float32,
    )
    solved = lax.psum(partial_value, "col").astype(jnp.bfloat16)
    pairs = [
        (
            broadcast(own_basis, "row", sources[band_slot]),
            broadcast(solved, "row", sources[band_slot]),
        )
        for band_slot in range(band_width)
    ]
    bases = [pair_now[0] for pair_now in pairs]
    weights = [pair_now[1] for pair_now in pairs]
    left_grams = []
    right_grams = []
    for band_slot in range(band_width):
        band_tile = band_tiles[band_slot]
        core_mat = cross_rows(solved, weights[band_slot])
        core_mat = jnp.where(band_tile < own_tile, core_mat, jnp.zeros_like(core_mat)).astype(
            jnp.bfloat16
        )
        update = jnp.dot(bases[band_slot], core_mat.T, preferred_element_type=jnp.float32).astype(
            jnp.bfloat16
        )
        trail_keep = (columns < rank_lookup(own_tile, band_tile))[None, :]
        kept_u = jnp.where(trail_keep, trail_u[0, band_slot], jnp.zeros_like(update))
        kept_v = jnp.where(trail_keep, trail_v[0, band_slot], jnp.zeros_like(update))
        left_stack = jnp.concatenate([kept_u, own_basis], axis=1)
        right_stack = jnp.concatenate([kept_v, -update], axis=1)
        left_grams.append(cross_rows(left_stack, left_stack))
        right_grams.append(cross_rows(right_stack, right_stack))
    return (jnp.stack(left_grams, axis=0)[None], jnp.stack(right_grams, axis=0)[None])


def solution(mesh):
    return jax.shard_map(
        shards,
        mesh=mesh,
        in_specs=(
            P("row", None, None),
            P("row", "col", None),
            P("row", "col"),
            P("row", "col", None, None),
            P("row", "col", None, None),
            P(),
            P(),
            P("col"),
        ),
        out_specs=(P("row", "col", None, None), P("row", "col", None, None)),
        check_vma=False,
    )
```

profile of v0, /device:TPU:0, one launch (start us, length us, event | category | flops | bytes accessed | tf_op | source)
XLA Modules:
  0.0 272.0 jit_solution(12180962195053194650)
XLA Ops:
  7.2 0.7 all-gather.2.cloned.1.call-update
  8.0 1.3 fusion.42
  9.3 2.6 fusion.31
  15.7 1.3 copy.11
  17.1 1.1 copy.15
  18.5 0.7 iota_compare_fusion
  20.4 0.8 select_reduce_fusion.2
  21.8 1.0 broadcast_select_fusion.3
  22.8 0.9 broadcast_select_fusion.1
  23.7 85.6 %all-gather.2.cloned.1.call-done = bf16[2560,1280]{1,0:T(8,128)(2,1)} async-done(((bf16[160,1280]{1,0:T(8,128)(2,1)}), bf16[2560,1280]{1,0:T(8,128)(2,1)}) %all-gather.2.cloned.1.call-update) | async-done | bytes 6553616 | tf_op jit(solution)/shard_map/all_gather | solution.py:40
  109.3 5.1 %convolution_bitcast_fusion = f32[2560,128]{0,1:T(8,128)S(1)} fusion(bf16[2560,1280]{1,0:T(8,128)(2,1)} %all-gather.2.cloned.1.call-done, bf16[1,1280,128]{2,1,0:T(8,128)(2,1)S(1)} %copy-done.5, pred[128]{0:T(512)(128)(4,1)S(1)} %iota_compare_fusion.2), kind=kOutput, calls=%fused_computation | convolution fusion | flops 839024640 | bytes 8192128 | tf_op jit(solution)/shard_map/dot_general | solution.py:39
  114.4 7.0 %all-reduce.5 = bf16[2560,128]{0,1:T(8,128)(2,1)S(1)} all-reduce(f32[2560,128]{0,1:T(8,128)S(1)} %convolution_bitcast_fusion), channel_id=1, replica_groups=mesh['row'=16,'col'=2] {'col'}, use_global_device_ids=true, to_apply=%region_6.7 | all-reduce | flops 327680 | bytes 1966080 | tf_op jit(solution)/shard_map/psum | solution.py:44
  121.4 1.2 broadcast_select_fusion.2
  122.6 1.4 fusion.40
  124.0 1.1 copy.17
  125.1 1.1 copy.18
  126.2 1.3 iota_compare_fusion.1
  127.5 1.2 bitcast_select_fusion.1
  130.5 0.8 maximum_bitcast_fusion
  131.4 126.5 %all-reduce.4.cloned.1.call-done = (bf16[2560,128]{0,1:T(8,128)(2,1)}, bf16[2560,128]{0,1:T(8,128)(2,1)}, bf16[2560,128]{0,1:T(8,128)(2,1)}, bf16[2560,128]{0,1:T(8,128)(2,1)}) async-done(((bf16[2560,128]{0,1:T(8,128)(2,1)}, bf16[2560,128]{0,1:T(8,128)(2,1)}, bf16[2560,128]{0,1:T(8,128)(2,1)}, bf16[2560,128]{0,1:T(8,128)(2,1)}), (bf16[2560,128]{0,1:T(8,128)(2,1)}, bf16[2560,128]{0,1:T(8,128)(2,1)}, ...) | async-done | bytes 2621456 | tf_op jit(solution)/shard_map/psum | solution.py:9
  257.9 3.0 %fusion = bf16[2560,128]{0,1:T(8,128)(2,1)} fusion(bf16[2560,128]{0,1:T(8,128)(2,1)} %get-tuple-element.10, bf16[2560,128]{0,1:T(8,128)(2,1)S(1)} %all-reduce.5, bf16[2560,128]{0,1:T(8,128)(2,1)} %get-tuple-element.11, pred[]{:T(512)S(6)} %lt.42), kind=kOutput, calls=%fused_computation.3 | convolution fusion | flops 169115648 | bytes 2621441 | tf_op jit(solution)/shard_map/dot_general | solution.py:62
  260.9 1.9 fusion.17
  262.9 0.9 fusion.1
  264.3 0.8 maximum_bitcast_fusion.1
  (26 shorter events, 4.6 us)
Async XLA Ops:
  7.2 9.8 %copy-start.2 = (bf16[1,2,2560,128]{3,2,1,0:T(8,128)(2,1)S(1)}, bf16[1,2,2560,128]{3,2,1,0:T(8,128)(2,1)}, u32[]{:S(2)}) copy-start(bf16[1,2,2560,128]{3,2,1,0:T(8,128)(2,1)} %param.11) | copy-start | bytes 3932164
  7.2 102.1 %all-gather.2.cloned.1.call-start = ((), (), s32[]{:S(2)}) async-start(), calls=%async_computation | async-start | bytes 6963200 | tf_op jit(solution)/shard_map/all_gather | solution.py:40
  7.9 250.0 %all-reduce.4.cloned.1.call-start = ((), (), s32[]{:S(2)}) async-start(), calls=%async_computation.1 | async-start | bytes 5242880 | tf_op jit(solution)/shard_map/psum | solution.py:9
  17.1 3.3 %copy-start.6 = (s32[16,16]{1,0:T(8,128)S(1)}, s32[16,16]{1,0:T(8,128)}, u32[]{:S(2)}) copy-start(s32[16,16]{1,0:T(8,128)} %param.13) | copy-start | bytes 3076
  21.8 87.5 %copy-start.5 = (bf16[1,1280,128]{2,1,0:T(8,128)(2,1)S(1)}, bf16[1,1280,128]{2,1,0:T(8,128)(2,1)}, u32[]{:S(2)}) copy-start(bf16[1,1280,128]{2,1,0:T(8,128)(2,1)} %param.9) | copy-start | bytes 983044
  125.1 2.4 copy-start
  128.7 1.1 copy-start.1
  260.9 1.9 copy-start.3
  260.9 1.9 copy-start.4
Sparse Core Ops, SparseCore 0:
  10.7 98.6 all-gather.1
  122.7 135.1 all-reduce.3
where the time goes:
time: 273 us; the launch traced here: 272 us
  waiting for transfers between devices  213 us (78%)
  between operations  18 us (7%)
  other arithmetic  13.4 us (5%)
  matrix products  12.6 us (5%)
  local copies, waits for them, and re-layouts  8.19 us (3%)
  blocking collectives  6.96 us (3%)
    psum x1, waiting for transfers between devices, broadcast(): return lax.psum(block, axis)  127 us
    all_gather x1, waiting for transfers between devices, shards(): lax.all_gather(linv, 'row', axis=0, tiled=True)  85.6 us
    psum x1, blocking collectives, shards(): solved = lax.psum(partial_value, 'col').astype(jnp.bfloat16)  6.96 us
  transfers between devices with their start and end apart: 2, of which 2 were waited for; matrix products, arithmetic and copies ran while one was open for 7% of the time, Pallas kernels for 0%

commit v1 on v0

--- a/solution.py
+++ b/solution.py
@@ -6,7 +6,8 @@
 
 def broadcast(block, axis, holder):
     block = jnp.where(lax.axis_index(axis) == holder, block, jnp.zeros_like(block))
-    return lax.psum(block, axis)
+    place_shifts_all = lambda panel, mesh_dim: jnp.sum(jax.lax.all_gather(panel, mesh_dim), 0)
+    return place_shifts_all(block, axis)
 
 
 def cross_rows(first, second):

time: 273 us -> 674 us (2.47)
  waiting for transfers between devices: 213 us -> 559 us
  other arithmetic: 13.4 us -> 45.2 us
  local copies, waits for them, and re-layouts: 8.19 us -> 32.8 us
    all_gather x0 -> x4, waiting for transfers between devices: none -> 468 us  [broadcast(): jax.lax.all_gather(panel, mesh_dim)]
    psum x1 -> x0, waiting for transfers between devices: 127 us -> none  [broadcast(): return lax.psum(block, axis)]
    reduce_sum x0 -> x4, other arithmetic: none -> 29.8 us  [broadcast(): jnp.sum(jax.lax.all_gather(panel, mesh_dim), 0)]
    unnamed x19, local copies, waits for them, and re-layouts: 5.42 us -> 28.7 us
  transfers between devices with their start and end apart: 2 -> 5, of which waited for: 2 -> 5; matrix products, arithmetic and copies ran while one was open for 7% -> 9% of each run, Pallas kernels for 0% -> 0%
where the time goes in v1:
time: 674 us
  waiting for transfers between devices  559 us (83%)
  other arithmetic  45.2 us (7%)
  local copies, waits for them, and re-layouts  32.8 us (5%)
  between operations  17.8 us (3%)
  matrix products  11.7 us (2%)
  blocking collectives  6.96 us (1%)
    all_gather x4, waiting for transfers between devices, broadcast(): jax.lax.all_gather(panel, mesh_dim)  468 us
    all_gather x1, waiting for transfers between devices, shards(): lax.all_gather(linv, 'row', axis=0, tiled=True)  88.9 us
    reduce_sum x4, other arithmetic, broadcast(): jnp.sum(jax.lax.all_gather(panel, mesh_dim), 0)  29.8 us
    unnamed x19, local copies, waits for them, and re-layouts  28.7 us
  transfers between devices with their start and end apart: 5, of which 5 were waited for; matrix products, arithmetic and copies ran while one was open for 9% of the time, Pallas kernels for 0%

profile of v1, /device:TPU:0, one launch (start us, length us, event | category | flops | bytes accessed | tf_op | source)
XLA Modules:
  0.0 673.6 jit_solution(1014953119871382980)
XLA Ops:
  7.9 1.3 fusion.42
  9.3 2.7 fusion.31
  15.2 1.5 select_reduce_fusion.2
  17.3 2.3 broadcast_select_fusion.4
  20.4 88.9 %all-gather.10.cloned.1.call-done = bf16[2560,1280]{1,0:T(8,128)(2,1)} async-done(((bf16[160,1280]{1,0:T(8,128)(2,1)}), bf16[2560,1280]{1,0:T(8,128)(2,1)}) %all-gather.10.cloned.1.call-update) | async-done | bytes 6553616 | tf_op jit(solution)/shard_map/all_gather | solution.py:41
  109.3 5.1 convolution_bitcast_fusion
  114.5 7.0 %all-reduce.1 = bf16[2560,128]{0,1:T(8,128)(2,1)S(1)} all-reduce(f32[2560,128]{0,1:T(8,128)S(1)} %convolution_bitcast_fusion), channel_id=1, replica_groups=mesh['row'=16,'col'=2] {'col'}, use_global_device_ids=true, to_apply=%region_6.7 | all-reduce | flops 327680 | bytes 1966080 | tf_op jit(solution)/shard_map/psum | solution.py:45
  121.4 1.2 broadcast_select_fusion.2
  126.1 1.4 fusion.41
  127.4 1.1 copy.20
  128.8 1.4 fusion.40
  132.4 1.3 iota_compare_fusion.1
  138.3 103.7 %all-gather.8.cloned.1.call-done = bf16[16,2560,128]{2,1,0:T(8,128)(2,1)} async-done(((bf16[1,2560,128]{2,1,0:T(8,128)(2,1)}), bf16[16,2560,128]{2,1,0:T(8,128)(2,1)}) %all-gather.8.cloned.1.call-update) | async-done | bytes 10485776 | tf_op jit(solution)/shard_map/all_gather | solution.py:9
  242.0 5.8 reduce_sum.107
  247.8 126.6 %all-gather.12.cloned.1.call-done = bf16[16,2560,128]{2,1,0:T(8,128)(2,1)} async-done(((bf16[1,2560,128]{2,1,0:T(8,128)(2,1)}), bf16[16,2560,128]{2,1,0:T(8,128)(2,1)}) %all-gather.12.cloned.1.call-update) | async-done | bytes 10485776 | tf_op jit(solution)/shard_map/all_gather | solution.py:9
  374.4 5.8 reduce_sum.110
  380.2 126.3 %all-gather.14.cloned.1.call-done = bf16[40960,128]{0,1:T(8,128)(2,1)} async-done(((bf16[2560,128]{0,1:T(8,128)(2,1)}), bf16[40960,128]{0,1:T(8,128)(2,1)}) %all-gather.14.cloned.1.call-update) | async-done | bytes 10485776 | tf_op jit(solution)/shard_map/all_gather | solution.py:9
  506.5 12.2 %copy.24 = bf16[16,8,16,2560]{3,2,1,0:T(8,128)(2,1)} copy(bf16[16,8,16,2560]{3,1,2,0:T(8,128)(2,1)} %bitcast.46) | data formatting | bytes 20971520
  518.7 9.1 %bitcast_reduce_fusion.1 = bf16[2560,128]{0,1:T(8,128)(2,1)S(1)} fusion(bf16[16,8,16,2560]{3,2,1,0:T(8,128)(2,1)} %copy.24), kind=kLoop, calls=%fused_computation.1 | loop fusion | flops 4915200 | bytes 11141120 | tf_op jit(solution)/shard_map/reduce_sum | solution.py:9
  527.8 111.7 %all-gather.16.cloned.1.call-done = bf16[40960,128]{0,1:T(8,128)(2,1)} async-done(((bf16[2560,128]{0,1:T(8,128)(2,1)}), bf16[40960,128]{0,1:T(8,128)(2,1)}) %all-gather.16.cloned.1.call-update) | async-done | bytes 10485776 | tf_op jit(solution)/shard_map/all_gather | solution.py:9
  639.5 11.9 %copy.25 = bf16[16,8,16,2560]{3,2,1,0:T(8,128)(2,1)} copy(bf16[16,8,16,2560]{3,1,2,0:T(8,128)(2,1)} %bitcast.47) | data formatting | bytes 20971520
  651.4 9.1 %bitcast_reduce_fusion = bf16[2560,128]{0,1:T(8,128)(2,1)S(1)} fusion(bf16[16,8,16,2560]{3,2,1,0:T(8,128)(2,1)} %copy.25), kind=kLoop, calls=%fused_computation | loop fusion | flops 4915200 | bytes 11141120 | tf_op jit(solution)/shard_map/reduce_sum | solution.py:9
  660.6 1.8 fusion
  662.3 2.3 fusion.17
  (39 shorter events, 14.4 us)
Async XLA Ops:
  7.2 102.2 %all-gather.10.cloned.1.call-start = ((), (), s32[]{:S(2)}) async-start(), calls=%async_computation.1 | async-start | bytes 6963200 | tf_op jit(solution)/shard_map/all_gather | solution.py:41
  7.9 234.1 %all-gather.8.cloned.1.call-start = ((), (), s32[]{:S(2)}) async-start(), calls=%async_computation | async-start | bytes 11141120 | tf_op jit(solution)/shard_map/all_gather | solution.py:9
  17.3 92.0 %copy-start.5 = (bf16[1,1280,128]{2,1,0:T(8,128)(2,1)S(1)}, bf16[1,1280,128]{2,1,0:T(8,128)(2,1)}, u32[]{:S(2)}) copy-start(bf16[1,1280,128]{2,1,0:T(8,128)(2,1)} %param.9) | copy-start | bytes 983044
  19.6 354.8 %all-gather.12.cloned.1.call-start = ((), (), s32[]{:S(2)}) async-start(), calls=%async_computation.2 | async-start | bytes 11141120 | tf_op jit(solution)/shard_map/all_gather | solution.py:9
  20.4 486.1 %all-gather.14.cloned.1.call-start = ((), (), s32[]{:S(2)}) async-start(), calls=%async_computation.3 | async-start | bytes 11141120 | tf_op jit(solution)/shard_map/all_gather | solution.py:9
  121.4 4.4 copy-start
  122.7 516.8 %all-gather.16.cloned.1.call-start = ((), (), s32[]{:S(2)}) async-start(), calls=%async_computation.4 | async-start | bytes 11141120 | tf_op jit(solution)/shard_map/all_gather | solution.py:9
  131.3 2.6 copy-start.1
  132.4 1.5 copy-start.3
  134.9 1.1 copy-start.2
  664.6 1.1 copy-start.4
Sparse Core Ops, SparseCore 0:
  10.7 98.6 all-gather.9
  112.0 129.9 all-gather.7
  244.7 129.6 all-gather.11
  377.0 129.4 all-gather.13
  509.1 130.4 all-gather.15
